TPU v7x, 512 devices: a whole 4x4x16 slice. The times are simulated.
512 devices in a mesh: seq: 128 (over y, z, core), tp: 4 (over x).
Axes of the slice: x: 4, y: 4, z: 16, core: 2. Of those that a mesh axis runs over, the one named last changes fastest.
Arguments:
- queries: float32 [16384, 2048], P('seq', 'tp'), may hold values from -6 to 6
- keys: float32 [16384, 2048], P('seq', 'tp'), may hold values from -6 to 6
- values: float32 [16384, 2048], P('seq', 'tp'), may hold values from -6 to 6
- out_weight: float32 [2048, 4096], P('seq', 'tp'), may hold values from -0.125 to 0.125
Outputs:
- mixed: float32 [16384, 4096], P('seq', 'tp')
All inputs are finite; a program needn't handle non-finite values.
Results may differ from a plain program's by a relative error of at most 0.0003.
Values sent between devices are 32-bit elements; how exact they have to be, the bound alone decides.
A program may use at most 128 MiB of HBM per device.

v0:
```python
import jax
import jax.numpy as jnp
from jax import lax
from jax.sharding import PartitionSpec as P

DH = 128


def prefix(part, axis, combine, identity):
    place = lax.axis_index(axis)
    gathered = jax.tree.map(lambda a: lax.all_gather(a, axis), part)
    state = jax.tree.map(lambda a, e: jnp.zeros_like(a) + jnp.asarray(e, a.dtype), part, identity)

    def one(step, state):
        return combine(
            state, jax.tree.map(lambda a: lax.dynamic_index_in_dim(a, step, 0, False), gathered)
        )

    return lax.fori_loop(0, place, one, state)


def features(inputs):
    return jnp.where(inputs > 0, inputs + 1.0, jnp.exp(jnp.minimum(inputs, 0.0)))


def combine(earlier, later):
    return (earlier[0] + later[0], earlier[1] + later[1])


def shards(queries, keys, values, out_weight):
    highest = lax.Precision.HIGHEST
    tok_rows = queries.shape[0]
    heads_here = queries.shape[1] // DH
    phi_queries = features(queries).reshape(tok_rows, heads_here, DH)
    phi_keys = features(keys).reshape(tok_rows, heads_here, DH)
    value_heads = values.reshape(tok_rows, heads_here, DH)
    memory_state = jnp.einsum("shd,she->hde", phi_keys, value_heads, precision=highest)
    key_total = jnp.sum(phi_keys, axis=0)
    identity = (jnp.zeros_like(memory_state), jnp.zeros_like(key_total))
    prior_state, prior_total = prefix((memory_state, key_total), "seq", combine, identity)
    causal_mask = jnp.arange(tok_rows)[:, None] >= jnp.arange(tok_rows)[None, :]
    scores = jnp.einsum("thd,shd->hts", phi_queries, phi_keys, precision=highest)
    scores = jnp.where(causal_mask[None], scores, 0.0)
    numerator = jnp.einsum("hts,shd->thd", scores, value_heads, precision=highest)
    numerator = numerator + jnp.einsum("thd,hde->the", phi_queries, prior_state, precision=highest)
    denominator = jnp.sum(scores, axis=2).T + jnp.einsum(
        "thd,hd->th", phi_queries, prior_total, precision=highest
    )
    attended = (numerator / denominator[:, :, None]).reshape(tok_rows, heads_here * DH)
    every_head = lax.all_gather(attended, "tp", axis=1, tiled=True)
    gathered = lax.all_gather(out_weight, "seq", axis=0, tiled=True)
    mixed = jnp.dot(every_head, gathered, precision=highest, preferred_element_type=jnp.float32)
    return mixed


def solution(mesh):
    return jax.shard_map(
        shards,
        mesh=mesh,
        in_specs=(P("seq", "tp"), P("seq", "tp"), P("seq", "tp"), P("seq", "tp")),
        out_specs=P("seq", "tp"),
        check_vma=False,
    )
```

profile of v0, /device:TPU:1, one launch (start us, length us, event | category | flops | bytes accessed | tf_op | source)
XLA Modules:
  0.0 401.2 jit_solution(6245858117362999715)
XLA Ops:
  6.5 0.0 copy-start
  6.5 0.0 all-gather.9.cloned.1.call-start
  6.5 1.1 fusion.7
  7.6 0.1 copy.31
  7.7 0.0 copy-done
  7.8 1.1 fusion.3
  8.8 0.0 all-gather.9.cloned.1.call-update
  8.9 0.0 all-gather.7.cloned.1.call-start
  8.9 0.7 all-gather.7.cloned.1.call-update
  9.6 0.0 all-gather.5.cloned.1.call-start
  9.7 1.0 exponential_select_fusion.1
  10.7 0.1 copy.30
  10.8 108.5 %all_gather.21 = f32[128,4,128]{2,1,0:T(4,128)S(1)} all-gather(f32[1,4,128]{2,1,0:T(4,128)S(1)} %bitcast.58), channel_id=1, replica_groups=mesh['seq'=128,'tp'=4] {'seq'}, dimensions={0}, use_global_device_ids=true | all-gather | bytes 264192 | tf_op jit(solution)/shard_map/all_gather | solution.py:11
  119.4 0.6 fusion.8
  120.0 0.6 convolution_bitcast_fusion.1
  120.6 90.9 %all-gather.9.cloned.1.call-done = f32[512,128,128]{2,1,0:T(8,128)} async-done(((f32[4,128,128]{2,1,0:T(8,128)}), f32[512,128,128]{2,1,0:T(8,128)}) %all-gather.9.cloned.1.call-update) | async-done | bytes 33554448 | tf_op jit(solution)/shard_map/all_gather | solution.py:11
  211.6 1.1 while.12
  211.6 1.0 bitcast_add_fusion.4
  212.6 0.3 fusion.9
  212.9 1.3 fusion.1
  214.3 0.0 all-gather.5.cloned.1.call-update
  214.3 143.7 %all-gather.7.cloned.1.call-done = f32[2048,1024]{1,0:T(8,128)} async-done(((f32[16,1024]{1,0:T(8,128)}), f32[2048,1024]{1,0:T(8,128)}) %all-gather.7.cloned.1.call-update) | async-done | bytes 8388624 | tf_op jit(solution)/shard_map/all_gather | solution.py:51
  358.0 27.5 %all-gather.5.cloned.1.call-done = f32[128,2048]{0,1:T(8,128)} async-done(((f32[128,512]{0,1:T(8,128)}), f32[128,2048]{0,1:T(8,128)}) %all-gather.5.cloned.1.call-update) | async-done | bytes 1048592 | tf_op jit(solution)/shard_map/all_gather | solution.py:50
  385.5 9.1 %fusion.10 = f32[128,1024]{1,0:T(8,128)} fusion(f32[128,2048]{0,1:T(8,128)} %all-gather.5.cloned.1.call-done, f32[2048,1024]{1,0:T(8,128)} %all-gather.7.cloned.1.call-done), kind=kOutput, calls=%fused_computation.19 | convolution fusion | flops 3221225472 | bytes 9961472 | tf_op jit(solution)/shard_map/dot_general | solution.py:52
  (5 shorter events, 0.1 us)
Async XLA Ops:
  6.5 1.2 copy-start
  6.5 205.0 %all-gather.9.cloned.1.call-start = ((), (), s32[]{:S(2)}) async-start(), calls=%async_computation.2 | async-start | bytes 33816576 | tf_op jit(solution)/shard_map/all_gather | solution.py:11
  8.9 349.1 %all-gather.7.cloned.1.call-start = ((), (), s32[]{:S(2)}) async-start(), calls=%async_computation.1 | async-start | bytes 8454144 | tf_op jit(solution)/shard_map/all_gather | solution.py:51
  9.6 375.9 %all-gather.5.cloned.1.call-start = ((), (), s32[]{:S(2)}) async-start(), calls=%async_computation | async-start | bytes 1310720 | tf_op jit(solution)/shard_map/all_gather | solution.py:50
Sparse Core Ops, SparseCore 0:
  10.5 200.9 all-gather.8
  214.7 143.2 all-gather.6
  360.1 25.3 all-gather.4
where the time goes:
time: 405 us; the launch traced here: 401 us
  waiting for transfers between devices  263 us (65%)
  blocking collectives  109 us (27%)
  between operations  13.2 us (3%)
  matrix products  13.1 us (3%)
    all_gather x1, waiting for transfers between devices, shards(): gathered = lax.all_gather(out_weight, 'seq', axis=0, tiled=True)  144 us
    all_gather x1, blocking collectives, prefix(): gathered = jax.tree.map(lambda a: lax.all_gather(a, axis), part)  109 us
    all_gather x1, waiting for transfers between devices, prefix(): gathered = jax.tree.map(lambda a: lax.all_gather(a, axis), part)  90.9 us
    all_gather x1, waiting for transfers between devices, shards(): every_head = lax.all_gather(attended, 'tp', axis=1, tiled=True)  27.5 us
    dot_general x1, matrix products, shards(): jnp.dot(every_head, gathered, precision=highest, preferred_element_type=j...  9.14 us
  transfers between devices with their start and end apart: 3, of which 3 were waited for; matrix products, arithmetic and copies ran while one was open for 1% of the time, Pallas kernels for 0%

commit v1 on v0

--- a/solution.py
+++ b/solution.py
@@ -47,7 +47,12 @@
         "thd,hd->th", phi_queries, prior_total, precision=highest
     )
     attended = (numerator / denominator[:, :, None]).reshape(tok_rows, heads_here * DH)
-    every_head = lax.all_gather(attended, "tp", axis=1, tiled=True)
+    ring = [attended]
+    for hop in range(3):
+        ring.append(lax.ppermute(ring[-1], "tp", [(dev, (dev + 1) % 4) for dev in range(4)]))
+    every_head = jnp.roll(
+        jnp.concatenate(ring[::-1], axis=1), (lax.axis_index("tp") + 1) * ring[0].shape[1], axis=1
+    )
     gathered = lax.all_gather(out_weight, "seq", axis=0, tiled=True)
     mixed = jnp.dot(every_head, gathered, precision=highest, preferred_element_type=jnp.float32)
     return mixed

time: 405 us -> 387 us (0.956)
  the two profiles are of different devices: /device:TPU:1 before, /device:TPU:504 now
where the time goes in v1:
time: 387 us; the launch traced here: 383 us
  other arithmetic  131 us (34%)
  waiting for transfers between devices  118 us (30%)
  blocking collectives  98 us (25%)
  between operations  13.6 us (4%)
  matrix products  11 us (3%)
  starting transfers between devices  7.5 us (2%)
    add x252, other arithmetic, combine(): return (earlier[0] + later[0], earlier[1] + later[1])  130 us
    all_gather x1, blocking collectives, prefix(): gathered = jax.tree.map(lambda a: lax.all_gather(a, axis), part)  98 us
    all_gather x1, waiting for transfers between devices, prefix(): gathered = jax.tree.map(lambda a: lax.all_gather(a, axis), part)  90.8 us
    ppermute x3, waiting for transfers between devices, shards(): lax.ppermute(ring[-1], 'tp', [(dev, (dev + 1) % 4) for dev in range(4)])  26.5 us
    dot_general x1, matrix products, shards(): jnp.dot(every_head, gathered, precision=highest, preferred_element_type=j...  7.79 us
  transfers between devices with their start and end apart: 5, of which 4 were waited for; matrix products, arithmetic and copies ran while one was open for 34% of the time, Pallas kernels for 0%

profile of v1, /device:TPU:504, one launch (start us, length us, event | category | flops | bytes accessed | tf_op | source)
XLA Modules:
  0.0 383.0 jit_solution(5748981289332566701)
XLA Ops:
  6.5 1.1 fusion.10
  7.8 1.1 fusion.5
  9.9 98.0 %all_gather.18 = f32[128,4,128]{2,1,0:T(4,128)S(1)} all-gather(f32[1,4,128]{2,1,0:T(4,128)S(1)} %bitcast.59), channel_id=1, replica_groups=mesh['seq'=128,'tp'=4] {'seq'}, dimensions={0}, use_global_device_ids=true | all-gather | bytes 264192 | tf_op jit(solution)/shard_map/all_gather | solution.py:11
  109.0 90.8 %all-gather.6.cloned.1.call-done = f32[512,128,128]{2,1,0:T(8,128)} async-done(((f32[4,128,128]{2,1,0:T(8,128)}), f32[512,128,128]{2,1,0:T(8,128)}) %all-gather.6.cloned.1.call-update) | async-done | bytes 33554448 | tf_op jit(solution)/shard_map/all_gather | solution.py:11
  199.8 133.4 %while.12 = (s32[]{:T(128)}, f32[4,128,128]{2,1,0:T(8,128)S(1)}, f32[4,128]{1,0:T(4,128)S(1)}, s32[]{:T(128)}, f32[128,4,128,128]{3,2,1,0:T(8,128)}, /*index=5*/...) while((s32[]{:T(128)}, f32[4,128,128]{2,1,0:T(8,128)S(1)}, f32[4,128]{1,0:T(4,128)S(1)}, s32[]{:T(128)}, ...), condition=%wide.region_2.3_spmd, body=%wide.region_1.2_spmd.sunk | while | flops 66053 | bytes 792711 | solution.py:19
  199.9 1.0 bitcast_add_fusion.4
  205.1 1.0 bitcast_add_fusion.4
  207.3 1.0 bitcast_add_fusion.4
  210.4 1.0 bitcast_add_fusion.4
  212.5 1.0 bitcast_add_fusion.4
  217.8 1.0 bitcast_add_fusion.4
  220.0 1.0 bitcast_add_fusion.4
  225.2 1.0 bitcast_add_fusion.4
  227.4 1.0 bitcast_add_fusion.4
  228.4 1.0 bitcast_add_fusion.4
  230.5 1.0 bitcast_add_fusion.4
  231.6 1.0 bitcast_add_fusion.4
  233.7 1.0 bitcast_add_fusion.4
  234.8 1.0 bitcast_add_fusion.4
  237.9 1.0 bitcast_add_fusion.4
  241.1 1.0 bitcast_add_fusion.4
  243.2 1.0 bitcast_add_fusion.4
  245.3 1.0 bitcast_add_fusion.4
  247.5 1.0 bitcast_add_fusion.4
  248.5 1.0 bitcast_add_fusion.4
  253.8 1.0 bitcast_add_fusion.4
  255.9 1.0 bitcast_add_fusion.4
  257.0 1.0 bitcast_add_fusion.4
  259.1 1.0 bitcast_add_fusion.4
  260.1 1.0 bitcast_add_fusion.4
  262.3 1.0 bitcast_add_fusion.4
  263.3 1.0 bitcast_add_fusion.4
  264.4 1.0 bitcast_add_fusion.4
  266.5 1.0 bitcast_add_fusion.4
  267.5 1.0 bitcast_add_fusion.4
  272.8 1.0 bitcast_add_fusion.4
  275.0 1.0 bitcast_add_fusion.4
  280.2 1.0 bitcast_add_fusion.4
  282.4 1.0 bitcast_add_fusion.4
  285.5 1.0 bitcast_add_fusion.4
  287.6 1.0 bitcast_add_fusion.4
  292.9 1.0 bitcast_add_fusion.4
  296.1 1.0 bitcast_add_fusion.4
  297.2 1.0 bitcast_add_fusion.4
  300.4 1.0 bitcast_add_fusion.4
  302.5 1.0 bitcast_add_fusion.4
  304.6 1.0 bitcast_add_fusion.4
  308.8 1.0 bitcast_add_fusion.4
  309.9 1.0 bitcast_add_fusion.4
  311.0 1.0 bitcast_add_fusion.4
  313.1 1.0 bitcast_add_fusion.4
  314.1 1.0 bitcast_add_fusion.4
  316.3 1.0 bitcast_add_fusion.4
  320.5 1.0 bitcast_add_fusion.4
  321.6 1.0 bitcast_add_fusion.4
  323.7 1.0 bitcast_add_fusion.4
  330.0 1.0 bitcast_add_fusion.4
  334.1 3.4 collective-permute-start
  337.5 8.6 %collective-permute-done = f32[128,512]{0,1:T(8,128)S(1)} collective-permute-done((f32[128,512]{0,1:T(8,128)S(1)}, f32[128,512]{0,1:T(8,128)S(1)}, u32[]{:S(2)}, u32[]{:S(2)}) %collective-permute-start) | collective-permute-done | bytes 262176 | tf_op jit(solution)/shard_map/ppermute | solution.py:52
  346.1 2.2 collective-permute-start.1
  348.3 9.3 %collective-permute-done.1 = f32[128,512]{0,1:T(8,128)S(1)} collective-permute-done((f32[128,512]{0,1:T(8,128)S(1)}, f32[128,512]{0,1:T(8,128)S(1)}, u32[]{:S(2)}, u32[]{:S(2)}) %collective-permute-start.1) | collective-permute-done | bytes 262176 | tf_op jit(solution)/shard_map/ppermute | solution.py:52
  357.6 1.9 collective-permute-start.2
  359.5 8.7 %collective-permute-done.2 = f32[128,512]{0,1:T(8,128)S(1)} collective-permute-done((f32[128,512]{0,1:T(8,128)S(1)}, f32[128,512]{0,1:T(8,128)S(1)}, u32[]{:S(2)}, u32[]{:S(2)}) %collective-permute-start.2) | collective-permute-done | bytes 262176 | tf_op jit(solution)/shard_map/ppermute | solution.py:52
  368.4 7.8 %fusion.2 = f32[128,1024]{1,0:T(8,128)} fusion(f32[2048,1024]{1,0:T(8,128)} %all-gather.4.cloned.1.call-done, f32[128,4096]{0,1:T(8,128)S(1)} %constant_dynamic-update-slice_fusion, s32[]{:T(128)S(6)} %select_n.34), kind=kOutput, calls=%fused_computation.7 | convolution fusion | flops 3221225472 | bytes 9961476 | tf_op jit(solution)/shard_map/dot_general | solution.py:57
  (228 shorter events, 80.3 us)
Async XLA Ops:
  6.5 1.2 copy-start
  6.5 3.1 copy-start.1
  6.5 193.3 %all-gather.6.cloned.1.call-start = ((), (), s32[]{:S(2)}) async-start(), calls=%async_computation.1 | async-start | bytes 33816576 | tf_op jit(solution)/shard_map/all_gather | solution.py:11
  8.9 359.5 %all-gather.4.cloned.1.call-start = ((), (), s32[]{:S(2)}) async-start(), calls=%async_computation | async-start | bytes 8454144 | tf_op jit(solution)/shard_map/all_gather | solution.py:56
  334.1 12.0 %collective-permute-start = (f32[128,512]{0,1:T(8,128)S(1)}, f32[128,512]{0,1:T(8,128)S(1)}, u32[]{:S(2)}, u32[]{:S(2)}) collective-permute-start(f32[128,512]{0,1:T(8,128)S(1)} %bitcast.54), channel_id=1, source_target_pairs={{0,1},{1,2},{2,3},{3,0},{4,5},{5,6},{6,7},{7,4},{8,9},{9,10},{10,1... | collective-permute-start | bytes 786440 | tf_op jit(solution)/shard_map/ppermute | solution.py:52
  346.1 11.4 %collective-permute-start.1 = (f32[128,512]{0,1:T(8,128)S(1)}, f32[128,512]{0,1:T(8,128)S(1)}, u32[]{:S(2)}, u32[]{:S(2)}) collective-permute-start(f32[128,512]{0,1:T(8,128)S(1)} %collective-permute-done), channel_id=1, source_target_pairs={{0,1},{1,2},{2,3},{3,0},{4,5},{5,6},{6,7},{7,4},{8,9},{9,10},{10,1... | collective-permute-start | bytes 786440 | tf_op jit(solution)/shard_map/ppermute | solution.py:52
  357.6 10.6 %collective-permute-start.2 = (f32[128,512]{0,1:T(8,128)S(1)}, f32[128,512]{0,1:T(8,128)S(1)}, u32[]{:S(2)}, u32[]{:S(2)}) collective-permute-start(f32[128,512]{0,1:T(8,128)S(1)} %collective-permute-done.1), channel_id=1, source_target_pairs={{0,1},{1,2},{2,3},{3,0},{4,5},{5,6},{6,7},{7,4},{8,9},{9,10},{10,1... | collective-permute-start | bytes 786440 | tf_op jit(solution)/shard_map/ppermute | solution.py:52
Sparse Core Ops, SparseCore 0:
  10.5 189.2 all-gather.5
  202.9 144.4 all-gather.3
